TPU v7x, 1024 devices: a whole 4x4x32 slice. The times are simulated.
1024 devices in a mesh: row: 64 (over z, core), col: 16 (over x, y).
Axes of the slice: x: 4, y: 4, z: 32, core: 2. Of those that a mesh axis runs over, the one named last changes fastest.
Arguments:
- spans: bfloat16 [32768, 768], P(('row', 'col')), may hold values from -10 to 10
- centroids: bfloat16 [8192, 768], P(('col', 'row')), may hold values from -10 to 10
- pattern: int32 [256, 16], P('row'), may hold values from 0 to 63, as said below
Outputs:
- new_centroids: bfloat16 [8192, 768], P(('col', 'row'))
- row_potential: float32 [32768], P('row')
- col_potential: float32 [8192], P('col')
Inputs may be any that keep to these rules, and one draw needn't show every extreme that they name: `pattern`: each row lists 16 distinct centroid blocks in rising order; row b always lists block b % 64; every centroid block is listed by some row.
All inputs are finite; a program needn't handle non-finite values.
Results may differ from a plain program's by a relative error of at most 0.0095.
Values may be sent and summed in bfloat16 or wider, within the bound.
A program may use at most 32 MiB of HBM per device.

v0:
```python
import math

import jax
import jax.numpy as jnp
from jax import lax
from jax.sharding import PartitionSpec as P

ITERS = 3


logit_scale = 0.0625
floor_value = -1e30


def per_device(spans, centroids, pattern):
    span_rows = lax.all_gather(spans, "col", axis=0, tiled=True)
    row_count = span_rows.shape[0]
    group_cols = centroids.shape[0] * lax.axis_size("row")
    all_centroids = lax.all_gather(centroids, "row", axis=0, tiled=True)
    scores = (
        lax.dot_general(
            span_rows, all_centroids, (((1,), (1,)), ((), ())), preferred_element_type=jnp.float32
        )
        * logit_scale
    )
    row_blocks = row_count // 128
    col_blocks = group_cols // 128
    block_ids = lax.axis_index("col") * col_blocks + jnp.arange(col_blocks, dtype=jnp.int32)
    listed = jnp.any(pattern[:, :, None] == block_ids[None, None, :], axis=1)
    allowed_cells = jnp.broadcast_to(
        listed[:, None, :, None], (row_blocks, 128, col_blocks, 128)
    ).reshape(row_count, group_cols)
    log_target = math.log(row_count * lax.axis_size("row") / (group_cols * lax.axis_size("col")))
    col_pot = jnp.zeros((group_cols,), jnp.float32)
    row_pot = jnp.zeros((row_count,), jnp.float32)
    for sweep in range(ITERS):
        shifted = jnp.where(allowed_cells, scores + col_pot[None, :], floor_value)
        row_high = jnp.max(shifted, axis=1)
        row_sum = jnp.sum(
            jnp.where(allowed_cells, jnp.exp(shifted - row_high[:, None]), 0.0), axis=1
        )
        whole_high = lax.pmax(row_high, "col")
        whole_sum = lax.psum(row_sum * jnp.exp(row_high - whole_high), "col")
        row_pot = -(whole_high + jnp.log(whole_sum))
        shifted = jnp.where(allowed_cells, scores + row_pot[:, None], floor_value)
        col_high = jnp.max(shifted, axis=0)
        col_sum = jnp.sum(
            jnp.where(allowed_cells, jnp.exp(shifted - col_high[None, :]), 0.0), axis=0
        )
        group_high = lax.pmax(col_high, "row")
        group_sum = lax.psum(col_sum * jnp.exp(col_high - group_high), "row")
        col_pot = log_target - (group_high + jnp.log(group_sum))
    weights = jnp.where(
        allowed_cells, jnp.exp(scores + row_pot[:, None] + col_pot[None, :]), 0.0
    ).astype(jnp.bfloat16)
    centroid_sum = lax.psum_scatter(
        lax.dot_general(
            weights, span_rows, (((0,), (0,)), ((), ())), preferred_element_type=jnp.float32
        ),
        "row",
        scatter_dimension=0,
        tiled=True,
    )
    mass_ratio = group_cols * lax.axis_size("col") / (row_count * lax.axis_size("row"))
    return ((centroid_sum * mass_ratio).astype(jnp.bfloat16), row_pot, col_pot)


def solution(mesh):
    placed = (P(("row", "col"), None), P(("col", "row"), None), P("row", None))
    return jax.shard_map(
        per_device,
        mesh=mesh,
        in_specs=placed,
        out_specs=(P(("col", "row"), None), P("row"), P("col")),
        check_vma=False,
    )
```

profile of v0, /device:TPU:1, one launch (start us, length us, event | category | flops | bytes accessed | tf_op | source)
XLA Modules:
  0.0 1076.4 jit_solution(4199485026371483575)
XLA Ops:
  7.2 0.0 reduce-scatter.2.cloned.1.call-start
  7.2 20.2 %all_gather.6 = bf16[512,768]{1,0:T(8,128)(2,1)S(1)} all-gather(bf16[32,768]{1,0:T(8,128)(2,1)} %param.3), channel_id=1, replica_groups=mesh['row'=64,'col'=16] {'col'}, dimensions={0}, use_global_device_ids=true | all-gather | bytes 835584 | tf_op jit(solution)/shard_map/all_gather | solution.py:16
  27.4 76.9 %all_gather.7 = bf16[512,768]{1,0:T(8,128)(2,1)S(1)} all-gather(bf16[8,768]{1,0:T(8,128)(2,1)} %param.4), channel_id=1, replica_groups=mesh['row'=64,'col'=16] {'row'}, dimensions={0}, use_global_device_ids=true | all-gather | bytes 798720 | tf_op jit(solution)/shard_map/all_gather | solution.py:19
  104.4 0.2 compare_reduce_fusion
  104.6 0.2 broadcast_in_dim.20
  104.8 0.7 fusion
  105.5 31.0 %pmax.42 = f32[512]{0:T(512)S(1)} all-reduce(f32[512]{0:T(512)S(1)} %get-tuple-element.3), channel_id=1, replica_groups=mesh['row'=64,'col'=16] {'col'}, use_global_device_ids=true, to_apply=%region_2.3 | all-reduce | flops 512 | bytes 4096 | tf_op jit(solution)/shard_map/pmax | solution.py:42
  136.5 0.5 select_reduce_fusion.5
  137.0 28.7 %psum.42 = f32[512]{0:T(512)S(1)} all-reduce(f32[512]{0:T(512)S(1)} %exponential_multiply_fusion.5), channel_id=1, replica_groups=mesh['row'=64,'col'=16] {'col'}, use_global_device_ids=true, to_apply=%region_4.5 | all-reduce | flops 512 | bytes 4096 | tf_op jit(solution)/shard_map/psum | solution.py:43
  165.8 0.2 fusion.2
  166.0 0.4 select_reduce_fusion.4
  166.4 103.6 %pmax.43 = f32[512]{0:T(512)S(1)} all-reduce(f32[512]{0:T(512)S(1)} %fusion.2), channel_id=1, replica_groups=mesh['row'=64,'col'=16] {'row'}, use_global_device_ids=true, to_apply=%region_6.7 | all-reduce | flops 512 | bytes 4096 | tf_op jit(solution)/shard_map/pmax | solution.py:50
  270.1 90.3 %psum.43 = f32[512]{0:T(512)S(1)} all-reduce(f32[512]{0:T(512)S(1)} %exponential_multiply_fusion.4), channel_id=1, replica_groups=mesh['row'=64,'col'=16] {'row'}, use_global_device_ids=true, to_apply=%region_8.9 | all-reduce | flops 512 | bytes 4096 | tf_op jit(solution)/shard_map/psum | solution.py:51
  360.4 0.3 fusion.3
  360.6 0.5 select_reduce_fusion.3
  361.1 30.2 %pmax.44 = f32[512]{0:T(512)S(1)} all-reduce(f32[512]{0:T(512)S(1)} %fusion.3), channel_id=1, replica_groups=mesh['row'=64,'col'=16] {'col'}, use_global_device_ids=true, to_apply=%region_10.11 | all-reduce | flops 512 | bytes 4096 | tf_op jit(solution)/shard_map/pmax | solution.py:42
  391.3 28.6 %psum.44 = f32[512]{0:T(512)S(1)} all-reduce(f32[512]{0:T(512)S(1)} %exponential_multiply_fusion.3), channel_id=1, replica_groups=mesh['row'=64,'col'=16] {'col'}, use_global_device_ids=true, to_apply=%region_12.13 | all-reduce | flops 512 | bytes 4096 | tf_op jit(solution)/shard_map/psum | solution.py:43
  419.9 0.2 fusion.4
  420.2 0.4 select_reduce_fusion.2
  420.6 104.5 %pmax.45 = f32[512]{0:T(512)S(1)} all-reduce(f32[512]{0:T(512)S(1)} %fusion.4), channel_id=1, replica_groups=mesh['row'=64,'col'=16] {'row'}, use_global_device_ids=true, to_apply=%region_14.15 | all-reduce | flops 512 | bytes 4096 | tf_op jit(solution)/shard_map/pmax | solution.py:50
  525.0 90.3 %psum.45 = f32[512]{0:T(512)S(1)} all-reduce(f32[512]{0:T(512)S(1)} %exponential_multiply_fusion.2), channel_id=1, replica_groups=mesh['row'=64,'col'=16] {'row'}, use_global_device_ids=true, to_apply=%region_16.17 | all-reduce | flops 512 | bytes 4096 | tf_op jit(solution)/shard_map/psum | solution.py:51
  615.3 0.3 fusion.5
  615.6 0.5 select_reduce_fusion.1
  616.1 30.2 %pmax.46 = f32[512]{0:T(512)S(1)} all-reduce(f32[512]{0:T(512)S(1)} %fusion.5), channel_id=1, replica_groups=mesh['row'=64,'col'=16] {'col'}, use_global_device_ids=true, to_apply=%region_18.19 | all-reduce | flops 512 | bytes 4096 | tf_op jit(solution)/shard_map/pmax | solution.py:42
  646.3 28.6 %psum.46 = f32[512]{0:T(512)S(1)} all-reduce(f32[512]{0:T(512)S(1)} %exponential_multiply_fusion.1), channel_id=1, replica_groups=mesh['row'=64,'col'=16] {'col'}, use_global_device_ids=true, to_apply=%region_20.21 | all-reduce | flops 512 | bytes 4096 | tf_op jit(solution)/shard_map/psum | solution.py:43
  674.9 0.2 fusion.1
  675.1 104.5 %pmax.47 = f32[512]{0:T(512)S(1)} all-reduce(f32[512]{0:T(512)S(1)} %fusion.1), channel_id=1, replica_groups=mesh['row'=64,'col'=16] {'row'}, use_global_device_ids=true, to_apply=%region_22.23 | all-reduce | flops 512 | bytes 4096 | tf_op jit(solution)/shard_map/pmax | solution.py:50
  779.6 0.4 select_reduce_fusion
  780.0 90.3 %psum.47 = f32[512]{0:T(512)S(1)} all-reduce(f32[512]{0:T(512)S(1)} %exponential_multiply_fusion), channel_id=1, replica_groups=mesh['row'=64,'col'=16] {'row'}, use_global_device_ids=true, to_apply=%region_24.25 | all-reduce | flops 512 | bytes 4096 | tf_op jit(solution)/shard_map/psum | solution.py:51
  870.3 2.0 fusion.6
  872.3 195.9 %reduce-scatter.2.cloned.1.call-done = f32[8,768]{1,0:T(8,128)} async-done(((f32[512,768]{1,0:T(8,128)}), f32[8,768]{1,0:T(8,128)}) %reduce-scatter.2.cloned.1.call-update) | async-done | bytes 24592 | tf_op jit(solution)/shard_map/reduce_scatter | solution.py:56
  1068.2 1.3 multiply_convert_fusion
  (20 shorter events, 0.1 us)
Async XLA Ops:
  7.2 97.2 %copy-start.2 = (s32[4,16]{1,0:T(4,128)S(1)}, s32[4,16]{1,0:T(4,128)}, u32[]{:S(2)}) copy-start(s32[4,16]{1,0:T(4,128)} %param.5) | copy-start | bytes 772
  7.2 1061.1 %reduce-scatter.2.cloned.1.call-start = ((), (), s32[]{:S(2)}) async-start(), calls=%async_computation.1 | async-start | bytes 1597440 | tf_op jit(solution)/shard_map/reduce_scatter | solution.py:56
  674.9 197.4 %copy-start = (f32[512]{0:T(512)}, f32[512]{0:T(512)S(1)}, u32[]{:S(2)}) copy-start(f32[512]{0:T(512)S(1)} %add_negate_fusion) | copy-start | bytes 6148
  870.3 2.0 copy-start.1
Sparse Core Ops, SparseCore 0:
  872.4 195.7 reduce-scatter.1
where the time goes:
time: 1080 us
  blocking collectives  858 us (79%)
  waiting for transfers between devices  196 us (18%)
  between operations  14.1 us (1%)
    pmax x3, blocking collectives, per_device(): group_high = lax.pmax(col_high, 'row')  313 us
    psum x3, blocking collectives, per_device(): group_sum = lax.psum(col_sum * jnp.exp(col_high - group_high), 'row')  271 us
    reduce_scatter x1, waiting for transfers between devices, per_device(): lax.psum_scatter(lax.dot_general(weights, span_rows, (((0,), (0,)), ((),...  196 us
    pmax x3, blocking collectives, per_device(): whole_high = lax.pmax(row_high, 'col')  91.5 us
    psum x3, blocking collectives, per_device(): whole_sum = lax.psum(row_sum * jnp.exp(row_high - whole_high), 'col')  85.9 us
    all_gather x1, blocking collectives, per_device(): all_centroids = lax.all_gather(centroids, 'row', axis=0, tiled=True)  76.9 us
  transfers between devices with their start and end apart: 1, of which 1 were waited for; matrix products, arithmetic and copies ran while one was open for 0% of the time, Pallas kernels for 0%

commit v1 on v0

v1 whole, which is shorter than its diff:
```python
import functools
import math

import jax
import jax.numpy as jnp
from jax import lax
from jax.experimental import pallas as pl
from jax.experimental.pallas import tpu as pltpu
from jax.sharding import PartitionSpec as P

MESH = pl.DeviceIdType.MESH
FLOOR = -1e30
SCALE = 0.0625
BLOCK = 128
NZ = 32
NXY = 16
STRIDE = 4
NA = NZ // STRIDE
WINDOW = (2, 1, 3)
SPANS, CENT_A, CENT_B, CENT_C = 0, 1, 2, 3
ROW, SIB, COL = 4, 7, 10
HALF, WIN, LAST = 13, 14, 15
NSEM = 16


def remote(src, dst, ssem, rsem, dev):
    return pltpu.make_async_remote_copy(
        src_ref=src, dst_ref=dst, send_sem=ssem, recv_sem=rsem, device_id=dev, device_id_type=MESH
    )


def drain(view, sem):
    pltpu.make_async_copy(view, view, sem).wait()


def kernel(
    log_target, target,
    sp_ref, ce_ref, pat_ref, newc_ref, rp_ref, cp_ref,
    spans_all, cent, plan, acc, half_out, half_in, win_out, win_in, last_out, last_in,
    rowx, sibx, sib_out, colx, total, ssem, rsem,
):
    r, c = lax.axis_index("row"), lax.axis_index("col")
    z, core = r // 2, r % 2
    a, b = z // STRIDE, z % STRIDE
    x, y = c // 4, c % 4
    other = 1 - core
    sibling = (z * 2 + other, c)

    def z_peer(d):
        return (((z + d) % NZ) * 2 + core, c)

    def xy_peer(k):
        return (r, ((x + k // 4) % 4) * 4 + (y + k % 4) % 4)

    def z_step(j):
        return 16 + ((j + 1) // 2) * (1 - 2 * (j % 2))

    def loop(n, fn):
        def step(i, carry):
            fn(i)
            return carry

        lax.fori_loop(0, n, step, 0)

    barrier = pltpu.get_barrier_semaphore()

    def greet(dev):
        pl.semaphore_signal(barrier, inc=1, device_id=dev, device_id_type=MESH)

    loop(NZ - 1, lambda j: greet(z_peer(z_step(j))))
    loop(NXY - 1, lambda j: greet(xy_peer(j + 1)))
    greet(sibling)
    pl.semaphore_wait(barrier, NZ - 1 + NXY - 1 + 1)

    for k in (4, 3, 5, 2, 6, 1, 7):
        remote(ce_ref, cent.at[a, b, core], ssem.at[CENT_A], rsem.at[CENT_A], z_peer(STRIDE * k)).start()
    loop(
        NXY - 1,
        lambda j: remote(
            sp_ref, spans_all.at[c], ssem.at[SPANS], rsem.at[SPANS], xy_peer((10 + j + (j + 10) // 16) % 16)
        ).start(),
    )
    spans_all[c] = sp_ref[...]
    cent[a, b, core] = ce_ref[...]
    drain(cent.at[pl.ds(0, NA - 1), 0, 0], rsem.at[CENT_A])
    for k in WINDOW:
        remote(
            cent.at[:, b, core], cent.at[:, b, core], ssem.at[CENT_B], rsem.at[CENT_B], z_peer(k if k < 3 else NZ - 1)
        ).start()
    drain(cent.at[:, pl.ds(0, 3), 0], rsem.at[CENT_B])
    remote(cent.at[:, :, core], cent.at[:, :, core], ssem.at[CENT_C], rsem.at[CENT_C], sibling).start()
    drain(spans_all.at[pl.ds(0, NXY - 1)], rsem.at[SPANS])
    drain(cent.at[:, :, 0], rsem.at[CENT_C])

    spans = spans_all[...].reshape(NXY * 32, -1)
    table = cent[...].astype(jnp.float32).reshape(NZ * 16, -1).astype(jnp.bfloat16)

    lanes = lax.broadcasted_iota(jnp.int32, (BLOCK, BLOCK), 1)
    diagonal = lax.broadcasted_iota(jnp.int32, (BLOCK, BLOCK), 0) == lanes

    def to_lanes(v):
        return jnp.sum(jnp.where(diagonal, v, 0.0), axis=0, keepdims=True)

    def to_rows(v):
        return jnp.sum(jnp.where(diagonal, v, 0.0), axis=1, keepdims=True)

    def wide(v):
        return jnp.concatenate([v[k : k + 1, :] for k in range(4)], axis=1)

    def rows_of(k):
        return pl.ds(k * BLOCK, BLOCK)

    def row_exchange(n):
        loop(
            NXY - 1,
            lambda j: remote(
                rowx.at[n, c], rowx.at[n, c], ssem.at[ROW + n], rsem.at[ROW + n], xy_peer((10 + j + (j + 10) // 16) % 16)
            ).start(),
        )
        drain(rowx.at[n, pl.ds(0, NXY - 1)], rsem.at[ROW + n])
        return rowx[n]

    def col_exchange_start(n, merge, part):
        for k in range(4):
            sib_out[n, k : k + 1, :] = part[:, k * BLOCK : (k + 1) * BLOCK]
        remote(sib_out.at[n], sibx.at[n], ssem.at[SIB + n], rsem.at[SIB + n], sibling).start()
        drain(sibx.at[n], rsem.at[SIB + n])
        colx[n, z] = merge(jnp.stack([sib_out[n], sibx[n]]))
        loop(
            NZ - 1,
            lambda j: remote(
                colx.at[n, z], colx.at[n, z], ssem.at[COL + n], rsem.at[COL + n], z_peer(z_step(j))
            ).start(),
        )

    def col_exchange_end(n):
        drain(colx.at[n, pl.ds(0, NZ - 1)], rsem.at[COL + n])
        return colx[n]

    def log_sum_exp(v):
        high = jnp.max(v, axis=0)
        return high + jnp.log(jnp.sum(jnp.exp(v - high[None]), axis=0))

    def add_up(v):
        return jnp.sum(v, axis=0)

    for i in range(4):
        listed = pat_ref[i : i + 1, :]
        scores = (
            lax.dot_general(
                spans[i * BLOCK : (i + 1) * BLOCK], table, (((1,), (1,)), ((), ())), preferred_element_type=jnp.float32
            )
            * SCALE
        )
        bias = jnp.concatenate(
            [
                jnp.broadcast_to(
                    jnp.max(jnp.where(listed == c * 4 + k, 0.0, FLOOR), axis=1, keepdims=True), (1, BLOCK)
                )
                for k in range(4)
            ],
            axis=1,
        )
        scores = scores + bias
        plan[rows_of(i), :] = scores
        high = jnp.max(scores, axis=1, keepdims=True)
        rowx[0, c, i : i + 1, :] = to_lanes(high + jnp.log(jnp.sum(jnp.exp(scores - high), axis=1, keepdims=True)))
    row_pot = -log_sum_exp(row_exchange(0))

    high = None
    for i in range(4):
        shifted = plan[rows_of(i), :] + to_rows(row_pot[i : i + 1, :])
        plan[rows_of(i), :] = shifted
        part = jnp.max(shifted, axis=0, keepdims=True)
        high = part if high is None else jnp.maximum(high, part)
    part = jnp.zeros_like(high)
    for i in range(4):
        part = part + jnp.sum(jnp.exp(plan[rows_of(i), :] - high), axis=0, keepdims=True)
    col_exchange_start(0, log_sum_exp, high + jnp.log(part))
    col_pot = log_target - log_sum_exp(col_exchange_end(0))

    for n in (1, 2):
        for i in range(4):
            if n == 1:
                p = jnp.exp(plan[rows_of(i), :] + wide(col_pot))
            else:
                p = plan[rows_of(i), :] * wide(col_scale)
            plan[rows_of(i), :] = p
            rowx[n, c, i : i + 1, :] = to_lanes(jnp.sum(p, axis=1, keepdims=True))
        row_sum = add_up(row_exchange(n))
        row_pot = row_pot - jnp.log(row_sum)
        row_scale = 1.0 / row_sum
        part = None
        for i in range(4):
            p = plan[rows_of(i), :] * to_rows(row_scale[i : i + 1, :])
            plan[rows_of(i), :] = p
            s = jnp.sum(p, axis=0, keepdims=True)
            part = s if part is None else part + s
        col_exchange_start(n, add_up, part)
        if n == 1:
            col_scale = target / add_up(col_exchange_end(n))
            col_pot = col_pot + jnp.log(col_scale)
    rp_ref[...] = row_pot

    sums = lax.dot_general(
        plan[...].astype(jnp.bfloat16), spans, (((0,), (0,)), ((), ())), preferred_element_type=jnp.float32
    )
    acc[...] = sums.reshape(acc.shape)
    half_out[...] = acc[:, :, other].astype(jnp.bfloat16)
    remote(half_out, half_in, ssem.at[HALF], rsem.at[HALF], sibling).start()
    drain(half_in, rsem.at[HALF])
    for s, k in enumerate(WINDOW):
        t = (b + k) % STRIDE
        win_out[s] = (acc[:, t, core] + half_in[:, t].astype(jnp.float32)).astype(jnp.bfloat16)
        remote(
            win_out.at[s], win_in.at[s], ssem.at[WIN], rsem.at[WIN], z_peer(k if k < 3 else NZ - 1)
        ).start()
    group = acc[:, b, core] + half_in[:, b].astype(jnp.float32)
    drain(win_in, rsem.at[WIN])
    for s in range(3):
        group = group + win_in[s].astype(jnp.float32)
    acc[:, b, core] = group
    last_out[...] = group.astype(jnp.bfloat16)
    for k in (4, 3, 5, 2, 6, 1, 7):
        remote(
            last_out.at[(a + k) % NA], last_in.at[k - 1], ssem.at[LAST], rsem.at[LAST], z_peer(STRIDE * k)
        ).start()

    col_sum = add_up(col_exchange_end(2))
    cp_ref[...] = col_pot + jnp.log(target / col_sum)
    total[...] = col_sum
    line = total[pl.ds(z // 8, 1), :]
    place = lax.broadcasted_iota(jnp.int32, (8, BLOCK), 1)
    wanted = lax.broadcasted_iota(jnp.int32, (8, BLOCK), 0) + (z % 8) * 16 + core * 8
    mine = jnp.sum(jnp.where(place == wanted, line, 0.0), axis=1, keepdims=True)

    drain(last_in, rsem.at[LAST])
    out = acc[a, b, core] + jnp.sum(last_in[...].astype(jnp.float32), axis=0)
    newc_ref[...] = (out / mine).astype(jnp.bfloat16)

    drain(spans_all.at[pl.ds(0, NXY - 1)], ssem.at[SPANS])
    drain(cent.at[pl.ds(0, NA - 1), 0, 0], ssem.at[CENT_A])
    drain(cent.at[:, pl.ds(0, 3), 0], ssem.at[CENT_B])
    drain(cent.at[:, :, 0], ssem.at[CENT_C])
    for n in range(3):
        drain(rowx.at[n, pl.ds(0, NXY - 1)], ssem.at[ROW + n])
        drain(sibx.at[n], ssem.at[SIB + n])
        drain(colx.at[n, pl.ds(0, NZ - 1)], ssem.at[COL + n])
    drain(half_in, ssem.at[HALF])
    drain(win_in, ssem.at[WIN])
    drain(last_in, ssem.at[LAST])


def solution(mesh):
    def per_device(spans, centroids, pattern):
        width = spans.shape[1]
        f32, bf16 = jnp.float32, jnp.bfloat16
        target = (spans.shape[0] * mesh.size) / (centroids.shape[0] * mesh.size)
        vmem = pl.BlockSpec(memory_space=pltpu.VMEM)
        new, row_pot, col_pot = pl.pallas_call(
            functools.partial(kernel, math.log(target), target),
            name="sinkhorn",
            out_shape=(
                jax.ShapeDtypeStruct((8, width), bf16),
                jax.ShapeDtypeStruct((4, BLOCK), f32),
                jax.ShapeDtypeStruct((4, BLOCK), f32),
            ),
            in_specs=[vmem] * 3,
            out_specs=(vmem,) * 3,
            scratch_shapes=[
                pltpu.VMEM((NXY, 32, width), bf16),
                pltpu.VMEM((NA, STRIDE, 2, 8, width), bf16),
                pltpu.VMEM((NXY * 32, NZ * 16), f32),
                pltpu.VMEM((NA, STRIDE, 2, 8, width), f32),
                pltpu.VMEM((NA, STRIDE, 8, width), bf16),
                pltpu.VMEM((NA, STRIDE, 8, width), bf16),
                pltpu.VMEM((3, NA, 8, width), bf16),
                pltpu.VMEM((3, NA, 8, width), bf16),
                pltpu.VMEM((NA, 8, width), bf16),
                pltpu.VMEM((NA - 1, 8, width), bf16),
                pltpu.VMEM((3, NXY, 4, BLOCK), f32),
                pltpu.VMEM((3, 4, BLOCK), f32),
                pltpu.VMEM((3, 4, BLOCK), f32),
                pltpu.VMEM((3, NZ, 4, BLOCK), f32),
                pltpu.VMEM((4, BLOCK), f32),
                pltpu.SemaphoreType.DMA((NSEM,)),
                pltpu.SemaphoreType.DMA((NSEM,)),
            ],
            compiler_params=pltpu.CompilerParams(
                collective_id=0, has_side_effects=True, vmem_limit_bytes=32 * 1024 * 1024
            ),
        )(spans, centroids, pattern)
        return new, row_pot.reshape(-1), col_pot.reshape(-1)

    return jax.shard_map(
        per_device,
        mesh=mesh,
        in_specs=(P(("row", "col"), None), P(("col", "row"), None), P("row", None)),
        out_specs=(P(("col", "row"), None), P("row"), P("col")),
        check_vma=False,
    )
```

time: 1080 us -> 128 us (0.12)
  the two profiles are of different devices: /device:TPU:1 before, /device:TPU:2 now
where the time goes in v1:
time: 128 us
  Pallas kernels  124 us (97%)
  local copies, waits for them, and re-layouts  3.94 us (3%)
    pallas_call x1, Pallas kernels, per_device(): pl.pallas_call(functools.partial(kernel, math.log(target), target), name=...  124 us
    unnamed x9, local copies, waits for them, and re-layouts  3.94 us

profile of v1, /device:TPU:2, one launch (start us, length us, event | category | flops | bytes accessed | tf_op | source)
XLA Modules:
  0.0 128.2 jit_solution(1841362522898568128)
XLA Ops:
  0.6 0.0 copy-start
  0.6 0.8 copy-done
  1.4 0.0 copy-start.1
  1.4 0.7 copy-done.1
  2.1 0.0 copy-start.2
  2.1 0.7 copy-done.2
  2.8 123.6 %sinkhorn.1 = (bf16[8,768]{1,0:T(8,128)(2,1)S(1)}, f32[4,128]{1,0:T(4,128)S(1)}, f32[4,128]{1,0:T(4,128)S(1)}) custom-call(bf16[32,768]{1,0:T(8,128)(2,1)S(1)} %copy-done, bf16[8,768]{1,0:T(8,128)(2,1)S(1)} %copy-done.1, s32[4,16]{1,0:T(4,128)S(1)} %copy-done.2), custom_call_target="tpu_custom_call" | custom-call | tf_op jit(solution)/shard_map/sinkhorn/pallas_call | solution.py:260
  126.4 0.6 copy.9
  127.0 0.6 copy.10
  127.6 0.6 copy.11
Async XLA Ops:
  0.6 0.8 copy-start
  1.4 0.7 copy-start.1
  2.1 0.7 copy-start.2

commit v2 on v1

--- a/solution.py
+++ b/solution.py
@@ -16,11 +16,12 @@
 NXY = 16
 STRIDE = 4
 NA = NZ // STRIDE
-WINDOW = (2, 1, 3)
-SPANS, CENT_A, CENT_B, CENT_C = 0, 1, 2, 3
+ORDER = (4, 3, 5, 2, 6, 1, 7, 0)
+SPANS, CENT_B, CENT_C, CENT_D = 0, 1, 2, 3
 ROW, SIB, COL = 4, 7, 10
-HALF, WIN, LAST = 13, 14, 15
-NSEM = 16
+LAST, UP, DOWN = 13, 14, 18
+HALF, WIN = 22, 30
+NSEM = 38
 
 
 def remote(src, dst, ssem, rsem, dev):
@@ -36,8 +37,8 @@
 def kernel(
     log_target, target,
     sp_ref, ce_ref, pat_ref, newc_ref, rp_ref, cp_ref,
-    spans_all, cent, plan, acc, half_out, half_in, win_out, win_in, last_out, last_in,
-    rowx, sibx, sib_out, colx, total, ssem, rsem,
+    spans_all, cent, pat, plan, acc, half_out, half_in, win_out, win_in, group, last_out, last_in,
+    rowx, sibx, sib_out, colx, total, ssem, rsem, lsem,
 ):
     r, c = lax.axis_index("row"), lax.axis_index("col")
     z, core = r // 2, r % 2
@@ -62,35 +63,57 @@
 
         lax.fori_loop(0, n, step, 0)
 
+    local = [
+        pltpu.make_async_copy(ce_ref, cent.at[a, b, core], lsem.at[0]),
+        pltpu.make_async_copy(sp_ref, spans_all.at[c], lsem.at[1]),
+        pltpu.make_async_copy(pat_ref, pat, lsem.at[2]),
+    ]
+    for copy in local:
+        copy.start()
+
     barrier = pltpu.get_barrier_semaphore()
 
     def greet(dev):
         pl.semaphore_signal(barrier, inc=1, device_id=dev, device_id_type=MESH)
 
-    loop(NZ - 1, lambda j: greet(z_peer(z_step(j))))
+    for k in (4, 28, 2, 30, 1, 31):
+        greet(z_peer(k))
     loop(NXY - 1, lambda j: greet(xy_peer(j + 1)))
     greet(sibling)
-    pl.semaphore_wait(barrier, NZ - 1 + NXY - 1 + 1)
-
-    for k in (4, 3, 5, 2, 6, 1, 7):
-        remote(ce_ref, cent.at[a, b, core], ssem.at[CENT_A], rsem.at[CENT_A], z_peer(STRIDE * k)).start()
+    pl.semaphore_wait(barrier, 6 + NXY - 1 + 1)
+    for copy in local:
+        copy.wait()
+
+    def pass_on(k, onward):
+        piece = cent.at[(a - k + NA) % NA, b, core]
+        if "up" in onward:
+            remote(piece, piece, ssem.at[UP + k], rsem.at[UP + k], z_peer(STRIDE)).start()
+        if "down" in onward:
+            remote(piece, piece, ssem.at[DOWN - k], rsem.at[DOWN - k], z_peer(NZ - STRIDE)).start()
+        for d in (2, 1, 31):
+            remote(piece, piece, ssem.at[CENT_B], rsem.at[CENT_B], z_peer(d)).start()
+
+    pass_on(0, ("up", "down"))
     loop(
         NXY - 1,
         lambda j: remote(
-            sp_ref, spans_all.at[c], ssem.at[SPANS], rsem.at[SPANS], xy_peer((10 + j + (j + 10) // 16) % 16)
+            spans_all.at[c], spans_all.at[c], ssem.at[SPANS], rsem.at[SPANS], xy_peer((10 + j + (j + 10) // 16) % 16)
         ).start(),
     )
-    spans_all[c] = sp_ref[...]
-    cent[a, b, core] = ce_ref[...]
-    drain(cent.at[pl.ds(0, NA - 1), 0, 0], rsem.at[CENT_A])
-    for k in WINDOW:
-        remote(
-            cent.at[:, b, core], cent.at[:, b, core], ssem.at[CENT_B], rsem.at[CENT_B], z_peer(k if k < 3 else NZ - 1)
-        ).start()
+    for k in (1, 2, 3, 4):
+        drain(cent.at[0, 0, 0], rsem.at[UP + k - 1])
+        pass_on(k, ("up",) if k < 4 else ())
+        if k < 4:
+            drain(cent.at[0, 0, 0], rsem.at[DOWN + k - 1])
+            pass_on(-k, ("down",) if k < 3 else ())
+    remote(cent.at[:, b, core], cent.at[:, b, core], ssem.at[CENT_C], rsem.at[CENT_C], sibling).start()
     drain(cent.at[:, pl.ds(0, 3), 0], rsem.at[CENT_B])
-    remote(cent.at[:, :, core], cent.at[:, :, core], ssem.at[CENT_C], rsem.at[CENT_C], sibling).start()
+    for k in (1, 2, 3):
+        t = (b + k) % STRIDE
+        remote(cent.at[:, t, core], cent.at[:, t, core], ssem.at[CENT_D], rsem.at[CENT_D], sibling).start()
     drain(spans_all.at[pl.ds(0, NXY - 1)], rsem.at[SPANS])
-    drain(cent.at[:, :, 0], rsem.at[CENT_C])
+    drain(cent.at[:, 0, 0], rsem.at[CENT_C])
+    drain(cent.at[:, pl.ds(0, 3), 0], rsem.at[CENT_D])
 
     spans = spans_all[...].reshape(NXY * 32, -1)
     table = cent[...].astype(jnp.float32).reshape(NZ * 16, -1).astype(jnp.bfloat16)
@@ -120,10 +143,12 @@
         drain(rowx.at[n, pl.ds(0, NXY - 1)], rsem.at[ROW + n])
         return rowx[n]
 
-    def col_exchange_start(n, merge, part):
+    def sibling_send(n, part):
         for k in range(4):
             sib_out[n, k : k + 1, :] = part[:, k * BLOCK : (k + 1) * BLOCK]
         remote(sib_out.at[n], sibx.at[n], ssem.at[SIB + n], rsem.at[SIB + n], sibling).start()
+
+    def col_send(n, merge):
         drain(sibx.at[n], rsem.at[SIB + n])
         colx[n, z] = merge(jnp.stack([sib_out[n], sibx[n]]))
         loop(
@@ -145,7 +170,7 @@
         return jnp.sum(v, axis=0)
 
     for i in range(4):
-        listed = pat_ref[i : i + 1, :]
+        listed = pat[i : i + 1, :]
         scores = (
             lax.dot_general(
                 spans[i * BLOCK : (i + 1) * BLOCK], table, (((1,), (1,)), ((), ())), preferred_element_type=jnp.float32
@@ -176,7 +201,8 @@
     part = jnp.zeros_like(high)
     for i in range(4):
         part = part + jnp.sum(jnp.exp(plan[rows_of(i), :] - high), axis=0, keepdims=True)
-    col_exchange_start(0, log_sum_exp, high + jnp.log(part))
+    sibling_send(0, high + jnp.log(part))
+    col_send(0, log_sum_exp)
     col_pot = log_target - log_sum_exp(col_exchange_end(0))
 
     for n in (1, 2):
@@ -196,8 +222,9 @@
             plan[rows_of(i), :] = p
             s = jnp.sum(p, axis=0, keepdims=True)
             part = s if part is None else part + s
-        col_exchange_start(n, add_up, part)
+        sibling_send(n, part)
         if n == 1:
+            col_send(n, add_up)
             col_scale = target / add_up(col_exchange_end(n))
             col_pot = col_pot + jnp.log(col_scale)
     rp_ref[...] = row_pot
@@ -206,25 +233,38 @@
         plan[...].astype(jnp.bfloat16), spans, (((0,), (0,)), ((), ())), preferred_element_type=jnp.float32
     )
     acc[...] = sums.reshape(acc.shape)
-    half_out[...] = acc[:, :, other].astype(jnp.bfloat16)
-    remote(half_out, half_in, ssem.at[HALF], rsem.at[HALF], sibling).start()
-    drain(half_in, rsem.at[HALF])
-    for s, k in enumerate(WINDOW):
-        t = (b + k) % STRIDE
-        win_out[s] = (acc[:, t, core] + half_in[:, t].astype(jnp.float32)).astype(jnp.bfloat16)
-        remote(
-            win_out.at[s], win_in.at[s], ssem.at[WIN], rsem.at[WIN], z_peer(k if k < 3 else NZ - 1)
-        ).start()
-    group = acc[:, b, core] + half_in[:, b].astype(jnp.float32)
-    drain(win_in, rsem.at[WIN])
-    for s in range(3):
-        group = group + win_in[s].astype(jnp.float32)
-    acc[:, b, core] = group
-    last_out[...] = group.astype(jnp.bfloat16)
-    for k in (4, 3, 5, 2, 6, 1, 7):
-        remote(
-            last_out.at[(a + k) % NA], last_in.at[k - 1], ssem.at[LAST], rsem.at[LAST], z_peer(STRIDE * k)
-        ).start()
+
+    def stop(d):
+        q = (z + d) % NZ
+        return q // STRIDE, q % STRIDE
+
+    stops = [stop(d) for d in (2, 1, 31)] + [(a, b)]
+    for i, k in enumerate(ORDER):
+        for s, (qa, qb) in enumerate(stops):
+            half_out[i, s] = acc[(qa + k) % NA, qb, other].astype(jnp.bfloat16)
+        remote(half_out.at[i], half_in.at[i], ssem.at[HALF + i], rsem.at[HALF + i], sibling).start()
+    for i, k in enumerate(ORDER):
+        drain(half_in.at[i], rsem.at[HALF + i])
+        for s, (qa, qb) in enumerate(stops):
+            both = acc[(qa + k) % NA, qb, core] + half_in[i, s].astype(jnp.float32)
+            if s == 3:
+                group[i] = both
+                continue
+            win_out[i, s] = both.astype(jnp.bfloat16)
+            remote(
+                win_out.at[i, s], win_in.at[i, s], ssem.at[WIN + i], rsem.at[WIN + i], z_peer((2, 1, 31)[s])
+            ).start()
+    col_send(2, add_up)
+    for i, k in enumerate(ORDER):
+        drain(win_in.at[i], rsem.at[WIN + i])
+        whole = group[i]
+        for s in range(3):
+            whole = whole + win_in[i, s].astype(jnp.float32)
+        if k == 0:
+            group[i] = whole
+            continue
+        last_out[i] = whole.astype(jnp.bfloat16)
+        remote(last_out.at[i], last_in.at[i], ssem.at[LAST], rsem.at[LAST], z_peer(STRIDE * k)).start()
 
     col_sum = add_up(col_exchange_end(2))
     cp_ref[...] = col_pot + jnp.log(target / col_sum)
@@ -235,19 +275,24 @@
     mine = jnp.sum(jnp.where(place == wanted, line, 0.0), axis=1, keepdims=True)
 
     drain(last_in, rsem.at[LAST])
-    out = acc[a, b, core] + jnp.sum(last_in[...].astype(jnp.float32), axis=0)
+    out = group[NA - 1] + jnp.sum(last_in[...].astype(jnp.float32), axis=0)
     newc_ref[...] = (out / mine).astype(jnp.bfloat16)
 
     drain(spans_all.at[pl.ds(0, NXY - 1)], ssem.at[SPANS])
-    drain(cent.at[pl.ds(0, NA - 1), 0, 0], ssem.at[CENT_A])
     drain(cent.at[:, pl.ds(0, 3), 0], ssem.at[CENT_B])
-    drain(cent.at[:, :, 0], ssem.at[CENT_C])
+    drain(cent.at[:, 0, 0], ssem.at[CENT_C])
+    drain(cent.at[:, pl.ds(0, 3), 0], ssem.at[CENT_D])
+    for k in range(4):
+        drain(cent.at[0, 0, 0], ssem.at[UP + k])
+    for k in range(3):
+        drain(cent.at[0, 0, 0], ssem.at[DOWN + k])
     for n in range(3):
         drain(rowx.at[n, pl.ds(0, NXY - 1)], ssem.at[ROW + n])
         drain(sibx.at[n], ssem.at[SIB + n])
         drain(colx.at[n, pl.ds(0, NZ - 1)], ssem.at[COL + n])
-    drain(half_in, ssem.at[HALF])
-    drain(win_in, ssem.at[WIN])
+    for i in range(NA):
+        drain(half_in.at[i], ssem.at[HALF + i])
+        drain(win_in.at[i], ssem.at[WIN + i])
     drain(last_in, ssem.at[LAST])
 
 
@@ -265,18 +310,20 @@
                 jax.ShapeDtypeStruct((4, BLOCK), f32),
                 jax.ShapeDtypeStruct((4, BLOCK), f32),
             ),
-            in_specs=[vmem] * 3,
+            in_specs=[pl.BlockSpec(memory_space=pltpu.HBM)] * 3,
             out_specs=(vmem,) * 3,
             scratch_shapes=[
                 pltpu.VMEM((NXY, 32, width), bf16),
                 pltpu.VMEM((NA, STRIDE, 2, 8, width), bf16),
+                pltpu.VMEM((4, 16), jnp.int32),
                 pltpu.VMEM((NXY * 32, NZ * 16), f32),
                 pltpu.VMEM((NA, STRIDE, 2, 8, width), f32),
-                pltpu.VMEM((NA, STRIDE, 8, width), bf16),
-                pltpu.VMEM((NA, STRIDE, 8, width), bf16),
-                pltpu.VMEM((3, NA, 8, width), bf16),
-                pltpu.VMEM((3, NA, 8, width), bf16),
-                pltpu.VMEM((NA, 8, width), bf16),
+                pltpu.VMEM((NA, 4, 8, width), bf16),
+                pltpu.VMEM((NA, 4, 8, width), bf16),
+                pltpu.VMEM((NA, 3, 8, width), bf16),
+                pltpu.VMEM((NA, 3, 8, width), bf16),
+                pltpu.VMEM((NA, 8, width), f32),
+                pltpu.VMEM((NA - 1, 8, width), bf16),
                 pltpu.VMEM((NA - 1, 8, width), bf16),
                 pltpu.VMEM((3, NXY, 4, BLOCK), f32),
                 pltpu.VMEM((3, 4, BLOCK), f32),
@@ -285,6 +332,7 @@
                 pltpu.VMEM((4, BLOCK), f32),
                 pltpu.SemaphoreType.DMA((NSEM,)),
                 pltpu.SemaphoreType.DMA((NSEM,)),
+                pltpu.SemaphoreType.DMA((3,)),
             ],
             compiler_params=pltpu.CompilerParams(
                 collective_id=0, has_side_effects=True, vmem_limit_bytes=32 * 1024 * 1024

time: 128 us -> 121 us (0.945)
  the two profiles are of different devices: /device:TPU:2 before, /device:TPU:1 now
where the time goes in v2:
time: 121 us; the launch traced here: 119 us
  Pallas kernels  115 us (95%)
  local copies, waits for them, and re-layouts  3.94 us (3%)
    pallas_call x1, Pallas kernels, per_device(): pl.pallas_call(functools.partial(kernel, math.log(target), target), name=...  115 us
    unnamed x9, local copies, waits for them, and re-layouts  3.94 us

profile of v2, /device:TPU:1, one launch (start us, length us, event | category | flops | bytes accessed | tf_op | source)
XLA Modules:
  0.0 119.2 jit_solution(9730890945080186378)
XLA Ops:
  0.6 0.0 copy-start
  0.6 0.8 copy-done
  1.4 0.0 copy-start.1
  1.4 0.7 copy-done.1
  2.1 0.0 copy-start.2
  2.1 0.7 copy-done.2
  2.8 114.6 %sinkhorn.1 = (bf16[8,768]{1,0:T(8,128)(2,1)S(1)}, f32[4,128]{1,0:T(4,128)S(1)}, f32[4,128]{1,0:T(4,128)S(1)}) custom-call(bf16[32,768]{1,0:T(8,128)(2,1)S(1)} %copy-done, bf16[8,768]{1,0:T(8,128)(2,1)S(1)} %copy-done.1, s32[4,16]{1,0:T(4,128)S(1)} %copy-done.2), custom_call_target="tpu_custom_call" | custom-call | tf_op jit(solution)/shard_map/sinkhorn/pallas_call | solution.py:305
  117.5 0.6 copy.9
  118.1 0.6 copy.10
  118.6 0.6 copy.11
Async XLA Ops:
  0.6 0.8 copy-start
  1.4 0.7 copy-start.1
  2.1 0.7 copy-start.2

commit v3 on v1

v3 whole, which is shorter than its diff:
```python
import functools
import math

import jax
import jax.numpy as jnp
from jax import lax
from jax.experimental import pallas as pl
from jax.experimental.pallas import tpu as pltpu
from jax.sharding import PartitionSpec as P

MESH = pl.DeviceIdType.MESH
FLOOR = -1e30
SCALE = 0.0625
BLOCK = 128
NZ = 32
NXY = 16
STRIDE = 4
NA = NZ // STRIDE
SPREAD = {0: (2, -2, 1, -1), 1: (2, 1, -1), -1: (-2, 1, -1), 2: (2, 1, -1), -2: (-2, 1, -1), 3: (3, 2, 1, -1), -3: (-3, -2, 1, -1), 4: ()}
ORDER = (4, 3, -3, 2, -2, 1, -1, 0)
WINDOW = [(k, d) for k in ORDER for d in SPREAD[k]]
SPANS, OTHER, PAT, CENT, POT, LAST = range(6)
ROW, COL, STOP, WIN = 6, 9, 12, 19
NSEM = 27


def remote(src, dst, ssem, rsem, dev):
    return pltpu.make_async_remote_copy(
        src_ref=src, dst_ref=dst, send_sem=ssem, recv_sem=rsem, device_id=dev, device_id_type=MESH
    )


def drain(view, sem):
    pltpu.make_async_copy(view, view, sem).wait()


def kernel(
    log_target, target,
    sp_ref, ce_ref, pat_ref, newc_ref, rp_ref, cp_ref,
    spans_all, cent, pat, plan, acc, win_out, win_in, last_out, last_in, rowx, colx, pots, total, ssem, rsem, lsem,
):
    r, c = lax.axis_index("row"), lax.axis_index("col")
    z, core = r // 2, r % 2
    a, b = z // STRIDE, z % STRIDE
    x, y = c // 4, c % 4
    other = 1 - core
    sibling = (z * 2 + other, c)

    def z_peer(d):
        return (((z + d + NZ) % NZ) * 2 + core, c)

    def far_first(i):
        return (2 + ((i + 1) // 2) * (1 - 2 * (i % 2))) % 4

    def xy_peer(j, flip):
        return (z * 2 + (core + flip) % 2, ((x + far_first(j // 4)) % 4) * 4 + (y + far_first(j % 4)) % 4)

    def z_step(j):
        return 16 + ((j + 1) // 2) * (1 - 2 * (j % 2))

    def loop(n, fn):
        def step(i, carry):
            fn(i)
            return carry

        lax.fori_loop(0, n, step, 0)

    local = [
        pltpu.make_async_copy(ce_ref, cent.at[a, b], lsem.at[0]),
        pltpu.make_async_copy(sp_ref, spans_all.at[core, c], lsem.at[1]),
        pltpu.make_async_copy(pat_ref, pat.at[core], lsem.at[2]),
    ]
    for copy in local:
        copy.start()

    barrier = pltpu.get_barrier_semaphore()

    def greet(dev):
        pl.semaphore_signal(barrier, inc=1, device_id=dev, device_id_type=MESH)

    near = [d * s for d in (8, 4, 3, 2, 1) for s in (1, -1)]
    for d in near:
        greet(z_peer(d))
    loop(NXY - 1, lambda j: greet(xy_peer(j, 0)))
    greet(sibling)
    pl.semaphore_wait(barrier, len(near) + NXY - 1 + 1)
    for copy in local:
        copy.wait()

    def chunk(k):
        return cent.at[(a - k + NA) % NA, b]

    def go(k, d, n):
        remote(chunk(k), chunk(k), ssem.at[STOP + n], rsem.at[STOP + n], z_peer(STRIDE * d)).start()

    def come(n):
        drain(chunk(0), rsem.at[STOP + n])

    def spread(k):
        for d in SPREAD[k]:
            remote(chunk(k), chunk(k), ssem.at[CENT], rsem.at[CENT], z_peer(d)).start()

    go(0, 2, 2)
    go(0, -2, 3)
    go(0, 1, 0)
    go(0, -1, 1)
    spread(0)
    mine = spans_all.at[core, c]
    loop(NXY - 1, lambda j: remote(mine, mine, ssem.at[SPANS], rsem.at[SPANS], xy_peer(j, 0)).start())
    remote(pat.at[core], pat.at[core], ssem.at[PAT], rsem.at[PAT], sibling).start()
    come(0)
    spread(1)
    come(1)
    spread(-1)
    come(2)
    go(2, 1, 4)
    come(3)
    go(-2, -1, 5)
    go(2 - 4 * core, 2 - 4 * core, 6)
    spread(2)
    spread(-2)
    drain(spans_all.at[0, pl.ds(0, NXY - 1)], rsem.at[SPANS])
    remote(spans_all.at[core], spans_all.at[core], ssem.at[OTHER], rsem.at[OTHER], sibling).start()
    come(4)
    spread(3)
    come(5)
    spread(-3)
    come(6)
    drain(pat.at[0], rsem.at[PAT])
    drain(spans_all.at[0], rsem.at[OTHER])
    drain(cent.at[:, pl.ds(0, 3)], rsem.at[CENT])

    spans = spans_all[...].reshape(2 * NXY * 32, -1)
    table = cent[...].astype(jnp.float32).reshape(NZ * 8, -1).astype(jnp.bfloat16)
    nblocks = 8

    down = lax.broadcasted_iota(jnp.int32, (BLOCK, BLOCK), 0)
    lanes = lax.broadcasted_iota(jnp.int32, (BLOCK, BLOCK), 1)
    diagonal = down == lanes

    def to_lanes(v):
        return jnp.sum(jnp.where(diagonal, v, 0.0), axis=0, keepdims=True)

    def to_rows(v):
        return jnp.sum(jnp.where(diagonal, v, 0.0), axis=1, keepdims=True)

    def wide(v):
        return jnp.concatenate([v[0:1, :], v[1:2, :]], axis=1)

    def rows_of(k):
        return pl.ds(k * BLOCK, BLOCK)

    me = c * 2 + core

    def row_exchange(n):
        part = rowx.at[n, me]
        loop(
            2 * (NXY - 1),
            lambda j: remote(part, part, ssem.at[ROW + n], rsem.at[ROW + n], xy_peer(j // 2, j % 2)).start(),
        )
        remote(part, part, ssem.at[ROW + n], rsem.at[ROW + n], sibling).start()
        drain(rowx.at[n, pl.ds(0, 2 * NXY - 1)], rsem.at[ROW + n])
        return rowx[n]

    def col_send(n, part):
        colx[n, z, 0:1, :] = part[:, :BLOCK]
        colx[n, z, 1:2, :] = part[:, BLOCK:]
        piece = colx.at[n, z]
        loop(NZ - 1, lambda j: remote(piece, piece, ssem.at[COL + n], rsem.at[COL + n], z_peer(z_step(j))).start())

    def col_receive(n):
        drain(colx.at[n, pl.ds(0, NZ - 1)], rsem.at[COL + n])
        return colx[n]

    def log_sum_exp(v):
        high = jnp.max(v, axis=0)
        return high + jnp.log(jnp.sum(jnp.exp(v - high[None]), axis=0))

    def add_up(v):
        return jnp.sum(v, axis=0)

    block_of = lax.broadcasted_iota(jnp.int32, (1, NZ * 8), 1) // 64
    for i in range(nblocks):
        listed = pat[i // 4, i % 4 : i % 4 + 1, :]
        bias = jnp.zeros((1, NZ * 8), jnp.float32)
        for k in range(4):
            cell = jnp.max(jnp.where(listed == c * 4 + k, 0.0, FLOOR), axis=1, keepdims=True)
            bias = bias + jnp.where(block_of == k, cell, 0.0)
        scores = (
            lax.dot_general(
                spans[i * BLOCK : (i + 1) * BLOCK], table, (((1,), (1,)), ((), ())), preferred_element_type=jnp.float32
            )
            * SCALE
            + bias
        )
        plan[rows_of(i), :] = scores
        high = jnp.max(scores, axis=1, keepdims=True)
        rowx[0, me, i : i + 1, :] = to_lanes(high + jnp.log(jnp.sum(jnp.exp(scores - high), axis=1, keepdims=True)))
    row_pot = -log_sum_exp(row_exchange(0))

    high = None
    for i in range(nblocks):
        shifted = plan[rows_of(i), :] + to_rows(row_pot[i : i + 1, :])
        plan[rows_of(i), :] = shifted
        part = jnp.max(shifted, axis=0, keepdims=True)
        high = part if high is None else jnp.maximum(high, part)
    part = jnp.zeros_like(high)
    for i in range(nblocks):
        part = part + jnp.sum(jnp.exp(plan[rows_of(i), :] - high), axis=0, keepdims=True)
    col_send(0, high + jnp.log(part))
    col_pot = log_target - log_sum_exp(col_receive(0))

    for n in (1, 2):
        for i in range(nblocks):
            if n == 1:
                p = jnp.exp(plan[rows_of(i), :] + wide(col_pot))
            else:
                p = plan[rows_of(i), :] * wide(col_scale)
            plan[rows_of(i), :] = p
            rowx[n, me, i : i + 1, :] = to_lanes(jnp.sum(p, axis=1, keepdims=True))
        row_sum = add_up(row_exchange(n))
        row_pot = row_pot - jnp.log(row_sum)
        row_scale = 1.0 / row_sum
        part = None
        for i in range(nblocks):
            p = plan[rows_of(i), :] * to_rows(row_scale[i : i + 1, :])
            plan[rows_of(i), :] = p
            s = jnp.sum(p, axis=0, keepdims=True)
            part = s if part is None else part + s
        if n == 1:
            col_send(n, part)
            col_scale = target / add_up(col_receive(n))
            col_pot = col_pot + jnp.log(col_scale)

    sums = lax.dot_general(
        plan[...].astype(jnp.bfloat16), spans, (((0,), (0,)), ((), ())), preferred_element_type=jnp.float32
    )
    acc[...] = sums.reshape(acc.shape)

    def send_last(i, k, whole):
        last_out[i] = whole.astype(jnp.bfloat16)
        remote(last_out.at[i], last_in.at[i], ssem.at[LAST], rsem.at[LAST], z_peer(-STRIDE * k)).start()

    send_last(0, 4, acc[(a + 4) % NA, b])
    for w, (k, d) in enumerate(WINDOW):
        stop = (z - d + NZ) % NZ
        win_out[w] = acc[(stop // STRIDE - k + NA) % NA, stop % STRIDE].astype(jnp.bfloat16)
        sem = WIN + ORDER.index(k)
        remote(win_out.at[w], win_in.at[w], ssem.at[sem], rsem.at[sem], z_peer(-d)).start()
    col_send(2, part)
    for i, k in enumerate(ORDER):
        if k == 4:
            continue
        lo = [w for w, (q, _) in enumerate(WINDOW) if q == k][0]
        drain(win_in.at[pl.ds(lo, len(SPREAD[k]))], rsem.at[WIN + i])
        whole = acc[(a - k + NA) % NA, b]
        for w in range(lo, lo + len(SPREAD[k])):
            whole = whole + win_in[w].astype(jnp.float32)
        if k != 0:
            send_last(i, k, whole)

    rp_ref[...] = jnp.where(core == 0, row_pot[:4, :], row_pot[4:, :])
    col_sum = add_up(col_receive(2))
    pots[core] = col_pot + jnp.log(target / col_sum)
    remote(pots.at[core], pots.at[core], ssem.at[POT], rsem.at[POT], sibling).start()
    total[...] = col_sum
    line = total[pl.ds(z // 16, 1), :]
    wanted = lax.broadcasted_iota(jnp.int32, (8, BLOCK), 0) + (z % 16) * 8
    place = lax.broadcasted_iota(jnp.int32, (8, BLOCK), 1)
    mass = jnp.sum(jnp.where(place == wanted, line, 0.0), axis=1, keepdims=True)
    drain(pots.at[0], rsem.at[POT])
    for i in range(4):
        line = jnp.zeros((1, BLOCK), jnp.float32)
        for q in range(2):
            take = (down == (i % 2) * 64 + (lanes // 16) * 8 + lanes % 8) & (lanes // 8 % 2 == q)
            line = line + jnp.sum(jnp.where(take, to_rows(pots[q, i // 2 : i // 2 + 1, :]), 0.0), axis=0, keepdims=True)
        cp_ref[i : i + 1, :] = line

    drain(last_in, rsem.at[LAST])
    out = whole + jnp.sum(last_in[...].astype(jnp.float32), axis=0)
    newc_ref[...] = (out / mass).astype(jnp.bfloat16)

    drain(spans_all.at[0, pl.ds(0, NXY - 1)], ssem.at[SPANS])
    drain(spans_all.at[0], ssem.at[OTHER])
    drain(pat.at[0], ssem.at[PAT])
    drain(cent.at[:, pl.ds(0, 3)], ssem.at[CENT])
    for n in range(7):
        drain(chunk(0), ssem.at[STOP + n])
    for n in range(3):
        drain(rowx.at[n, pl.ds(0, 2 * NXY - 1)], ssem.at[ROW + n])
        drain(colx.at[n, pl.ds(0, NZ - 1)], ssem.at[COL + n])
    for i, k in enumerate(ORDER):
        if k != 4:
            drain(win_in.at[pl.ds(0, len(SPREAD[k]))], ssem.at[WIN + i])
    drain(pots.at[0], ssem.at[POT])
    drain(last_in, ssem.at[LAST])


def solution(mesh):
    def per_device(spans, centroids, pattern):
        width = spans.shape[1]
        f32, bf16 = jnp.float32, jnp.bfloat16
        target = (spans.shape[0] * mesh.size) / (centroids.shape[0] * mesh.size)
        args = [pltpu.with_memory_space_constraint(v, pltpu.HBM) for v in (spans, centroids, pattern)]
        vmem = pl.BlockSpec(memory_space=pltpu.VMEM)
        new, row_pot, col_pot = pl.pallas_call(
            functools.partial(kernel, math.log(target), target),
            name="sinkhorn",
            out_shape=(
                jax.ShapeDtypeStruct((8, width), bf16),
                jax.ShapeDtypeStruct((4, BLOCK), f32),
                jax.ShapeDtypeStruct((4, BLOCK), f32),
            ),
            in_specs=[pl.BlockSpec(memory_space=pltpu.HBM)] * 3,
            out_specs=(vmem,) * 3,
            scratch_shapes=[
                pltpu.VMEM((2, NXY, 32, width), bf16),
                pltpu.VMEM((NA, STRIDE, 8, width), bf16),
                pltpu.VMEM((2, 4, 16), jnp.int32),
                pltpu.VMEM((2 * NXY * 32, NZ * 8), f32),
                pltpu.VMEM((NA, STRIDE, 8, width), f32),
                pltpu.VMEM((len(WINDOW), 8, width), bf16),
                pltpu.VMEM((len(WINDOW), 8, width), bf16),
                pltpu.VMEM((NA - 1, 8, width), bf16),
                pltpu.VMEM((NA - 1, 8, width), bf16),
                pltpu.VMEM((3, 2 * NXY, 8, BLOCK), f32),
                pltpu.VMEM((3, NZ, 2, BLOCK), f32),
                pltpu.VMEM((2, 2, BLOCK), f32),
                pltpu.VMEM((2, BLOCK), f32),
                pltpu.SemaphoreType.DMA((NSEM,)),
                pltpu.SemaphoreType.DMA((NSEM,)),
                pltpu.SemaphoreType.DMA((3,)),
            ],
            compiler_params=pltpu.CompilerParams(
                collective_id=0, has_side_effects=True, vmem_limit_bytes=32 * 1024 * 1024
            ),
        )(*args)
        return new, row_pot.reshape(-1), col_pot.reshape(-1)

    return jax.shard_map(
        per_device,
        mesh=mesh,
        in_specs=(P(("row", "col"), None), P(("col", "row"), None), P("row", None)),
        out_specs=(P(("col", "row"), None), P("row"), P("col")),
        check_vma=False,
    )
```

time: 128 us -> 115 us (0.90)
  the two profiles are of different devices: /device:TPU:2 before, /device:TPU:1 now
where the time goes in v3:
time: 115 us
  Pallas kernels  113 us (98%)
  local copies, waits for them, and re-layouts  1.76 us (2%)
    pallas_call x1, Pallas kernels, per_device(): pl.pallas_call(functools.partial(kernel, math.log(target), target), name=...  113 us

profile of v3, /device:TPU:1, one launch (start us, length us, event | category | flops | bytes accessed | tf_op | source)
XLA Modules:
  0.0 115.3 jit_solution(415311457827770490)
XLA Ops:
  0.6 112.9 %sinkhorn.1 = (bf16[8,768]{1,0:T(8,128)(2,1)S(1)}, f32[4,128]{1,0:T(4,128)S(1)}, f32[4,128]{1,0:T(4,128)S(1)}) custom-call(bf16[32,768]{1,0:T(8,128)(2,1)} %sp_ref.1, bf16[8,768]{1,0:T(8,128)(2,1)} %ce_ref.1, s32[4,16]{1,0:T(4,128)} %pat_ref.1), custom_call_target="tpu_custom_call" | custom-call | tf_op jit(solution)/shard_map/sinkhorn/pallas_call | solution.py:306
  113.5 0.6 copy.9
  114.1 0.6 copy.10
  114.7 0.6 copy.11

commit v4 on v3

--- a/solution.py
+++ b/solution.py
@@ -37,7 +37,7 @@
 def kernel(
     log_target, target,
     sp_ref, ce_ref, pat_ref, newc_ref, rp_ref, cp_ref,
-    spans_all, cent, pat, plan, acc, win_out, win_in, last_out, last_in, rowx, colx, pots, total, ssem, rsem, lsem,
+    spans_all, cent, pat, plan, acc, win_out, win_in, last_out, last_in, rowx, colx, pots, total, ssem, rsem, lsem, hsem,
 ):
     r, c = lax.axis_index("row"), lax.axis_index("col")
     z, core = r // 2, r % 2
@@ -78,12 +78,14 @@
     def greet(dev):
         pl.semaphore_signal(barrier, inc=1, device_id=dev, device_id_type=MESH)
 
-    near = [d * s for d in (8, 4, 3, 2, 1) for s in (1, -1)]
+    near = [d * s for d in (4, 3, 2, 1) for s in (1, -1)]
     for d in near:
         greet(z_peer(d))
     loop(NXY - 1, lambda j: greet(xy_peer(j, 0)))
     greet(sibling)
     pl.semaphore_wait(barrier, len(near) + NXY - 1 + 1)
+    for d in (STRIDE, -STRIDE):
+        pl.semaphore_signal(hsem, inc=1, device_id=z_peer(d), device_id_type=MESH)
     for copy in local:
         copy.wait()
 
@@ -100,30 +102,31 @@
         for d in SPREAD[k]:
             remote(chunk(k), chunk(k), ssem.at[CENT], rsem.at[CENT], z_peer(d)).start()
 
-    go(0, 2, 2)
-    go(0, -2, 3)
     go(0, 1, 0)
     go(0, -1, 1)
     spread(0)
     mine = spans_all.at[core, c]
     loop(NXY - 1, lambda j: remote(mine, mine, ssem.at[SPANS], rsem.at[SPANS], xy_peer(j, 0)).start())
     remote(pat.at[core], pat.at[core], ssem.at[PAT], rsem.at[PAT], sibling).start()
+    pl.semaphore_wait(hsem, 2)
     come(0)
+    go(1, 2, 4)
+    go(1, 1, 2)
     spread(1)
     come(1)
+    go(-1, -2, 5)
+    go(-1, -1, 3)
     spread(-1)
     come(2)
-    go(2, 1, 4)
+    spread(2)
     come(3)
-    go(-2, -1, 5)
-    go(2 - 4 * core, 2 - 4 * core, 6)
-    spread(2)
     spread(-2)
     drain(spans_all.at[0, pl.ds(0, NXY - 1)], rsem.at[SPANS])
     remote(spans_all.at[core], spans_all.at[core], ssem.at[OTHER], rsem.at[OTHER], sibling).start()
     come(4)
+    come(5)
+    go(3 - 6 * core, 1 - 2 * core, 6)
     spread(3)
-    come(5)
     spread(-3)
     come(6)
     drain(pat.at[0], rsem.at[PAT])
@@ -232,6 +235,7 @@
             col_scale = target / add_up(col_receive(n))
             col_pot = col_pot + jnp.log(col_scale)
 
+    col_send(2, part)
     sums = lax.dot_general(
         plan[...].astype(jnp.bfloat16), spans, (((0,), (0,)), ((), ())), preferred_element_type=jnp.float32
     )
@@ -242,15 +246,17 @@
         remote(last_out.at[i], last_in.at[i], ssem.at[LAST], rsem.at[LAST], z_peer(-STRIDE * k)).start()
 
     send_last(0, 4, acc[(a + 4) % NA, b])
-    for w, (k, d) in enumerate(WINDOW):
-        stop = (z - d + NZ) % NZ
-        win_out[w] = acc[(stop // STRIDE - k + NA) % NA, stop % STRIDE].astype(jnp.bfloat16)
-        sem = WIN + ORDER.index(k)
-        remote(win_out.at[w], win_in.at[w], ssem.at[sem], rsem.at[sem], z_peer(-d)).start()
-    col_send(2, part)
-    for i, k in enumerate(ORDER):
-        if k == 4:
-            continue
+
+    def send_window(*steps):
+        for w, (k, d) in enumerate(WINDOW):
+            if k in steps:
+                stop = (z - d + NZ) % NZ
+                win_out[w] = acc[(stop // STRIDE - k + NA) % NA, stop % STRIDE].astype(jnp.bfloat16)
+                sem = WIN + ORDER.index(k)
+                remote(win_out.at[w], win_in.at[w], ssem.at[sem], rsem.at[sem], z_peer(-d)).start()
+
+    def gather_window(k):
+        i = ORDER.index(k)
         lo = [w for w, (q, _) in enumerate(WINDOW) if q == k][0]
         drain(win_in.at[pl.ds(lo, len(SPREAD[k]))], rsem.at[WIN + i])
         whole = acc[(a - k + NA) % NA, b]
@@ -258,6 +264,19 @@
             whole = whole + win_in[w].astype(jnp.float32)
         if k != 0:
             send_last(i, k, whole)
+        return whole
+
+    send_window(3, -3)
+    send_window(2, -2)
+    gather_window(3)
+    gather_window(-3)
+    send_window(1, -1)
+    gather_window(2)
+    gather_window(-2)
+    send_window(0)
+    gather_window(1)
+    gather_window(-1)
+    whole = gather_window(0)
 
     rp_ref[...] = jnp.where(core == 0, row_pot[:4, :], row_pot[4:, :])
     col_sum = add_up(col_receive(2))
@@ -330,6 +349,7 @@
                 pltpu.SemaphoreType.DMA((NSEM,)),
                 pltpu.SemaphoreType.DMA((NSEM,)),
                 pltpu.SemaphoreType.DMA((3,)),
+                pltpu.SemaphoreType.REGULAR,
             ],
             compiler_params=pltpu.CompilerParams(
                 collective_id=0, has_side_effects=True, vmem_limit_bytes=32 * 1024 * 1024

time: 115 us -> 107 us (0.930)
  Pallas kernels: 113 us -> 104 us
    pallas_call x1, Pallas kernels: 113 us -> 104 us  [per_device(): pl.pallas_call(functools.partial(kernel, math.log(target), target), name=...]
where the time goes in v4:
time: 107 us; the launch traced here: 106 us
  Pallas kernels  104 us (97%)
  local copies, waits for them, and re-layouts  1.76 us (2%)
    pallas_call x1, Pallas kernels, per_device(): pl.pallas_call(functools.partial(kernel, math.log(target), target), name=...  104 us

profile of v4, /device:TPU:1, one launch (start us, length us, event | category | flops | bytes accessed | tf_op | source)
XLA Modules:
  0.0 106.4 jit_solution(2964217097201543289)
XLA Ops:
  0.6 104.0 %sinkhorn.1 = (bf16[8,768]{1,0:T(8,128)(2,1)S(1)}, f32[4,128]{1,0:T(4,128)S(1)}, f32[4,128]{1,0:T(4,128)S(1)}) custom-call(bf16[32,768]{1,0:T(8,128)(2,1)} %sp_ref.1, bf16[8,768]{1,0:T(8,128)(2,1)} %ce_ref.1, s32[4,16]{1,0:T(4,128)} %pat_ref.1), custom_call_target="tpu_custom_call" | custom-call | tf_op jit(solution)/shard_map/sinkhorn/pallas_call | solution.py:325
  104.7 0.6 copy.9
  105.3 0.6 copy.10
  105.9 0.6 copy.11

commit v5 on v4

--- a/solution.py
+++ b/solution.py
@@ -21,7 +21,8 @@
 WINDOW = [(k, d) for k in ORDER for d in SPREAD[k]]
 SPANS, OTHER, PAT, CENT, POT, LAST = range(6)
 ROW, COL, STOP, WIN = 6, 9, 12, 19
-NSEM = 27
+COLW, COLF = 27, 28
+NSEM = 29
 
 
 def remote(src, dst, ssem, rsem, dev):
@@ -36,9 +37,10 @@
 
 def kernel(
     log_target, target,
-    sp_ref, ce_ref, pat_ref, newc_ref, rp_ref, cp_ref,
-    spans_all, cent, pat, plan, acc, win_out, win_in, last_out, last_in, rowx, colx, pots, total, ssem, rsem, lsem, hsem,
+    sp_ref, ce_ref, pat_ref, out_ref,
+    spans_all, cent, pat, plan, acc, win_out, win_in, last_out, last_in, rowx, colx, colw, colf, pots, total, ssem, rsem, lsem, hsem,
 ):
+    width = sp_ref.shape[1]
     r, c = lax.axis_index("row"), lax.axis_index("col")
     z, core = r // 2, r % 2
     a, b = z // STRIDE, z % STRIDE
@@ -235,7 +237,11 @@
             col_scale = target / add_up(col_receive(n))
             col_pot = col_pot + jnp.log(col_scale)
 
-    col_send(2, part)
+    colw[3, 0:1, :] = part[:, :BLOCK]
+    colw[3, 1:2, :] = part[:, BLOCK:]
+    for i, d in enumerate((2, 1, -1)):
+        remote(colw.at[3], colw.at[i], ssem.at[COLW], rsem.at[COLW], z_peer(d)).start()
+
     sums = lax.dot_general(
         plan[...].astype(jnp.bfloat16), spans, (((0,), (0,)), ((), ())), preferred_element_type=jnp.float32
     )
@@ -268,6 +274,10 @@
 
     send_window(3, -3)
     send_window(2, -2)
+    drain(colw.at[pl.ds(0, 3)], rsem.at[COLW])
+    colf[NA - 1] = add_up(colw[...])
+    for i, k in enumerate((4, 3, -3, 2, -2, 1, -1)):
+        remote(colf.at[NA - 1], colf.at[i], ssem.at[COLF], rsem.at[COLF], z_peer(-STRIDE * k)).start()
     gather_window(3)
     gather_window(-3)
     send_window(1, -1)
@@ -278,8 +288,9 @@
     gather_window(-1)
     whole = gather_window(0)
 
-    rp_ref[...] = jnp.where(core == 0, row_pot[:4, :], row_pot[4:, :])
-    col_sum = add_up(col_receive(2))
+    out_ref[0:4, width:] = jnp.where(core == 0, row_pot[:4, :], row_pot[4:, :])
+    drain(colf.at[pl.ds(0, NA - 1)], rsem.at[COLF])
+    col_sum = add_up(colf[...])
     pots[core] = col_pot + jnp.log(target / col_sum)
     remote(pots.at[core], pots.at[core], ssem.at[POT], rsem.at[POT], sibling).start()
     total[...] = col_sum
@@ -293,11 +304,11 @@
         for q in range(2):
             take = (down == (i % 2) * 64 + (lanes // 16) * 8 + lanes % 8) & (lanes // 8 % 2 == q)
             line = line + jnp.sum(jnp.where(take, to_rows(pots[q, i // 2 : i // 2 + 1, :]), 0.0), axis=0, keepdims=True)
-        cp_ref[i : i + 1, :] = line
+        out_ref[4 + i : 5 + i, width:] = line
 
     drain(last_in, rsem.at[LAST])
     out = whole + jnp.sum(last_in[...].astype(jnp.float32), axis=0)
-    newc_ref[...] = (out / mass).astype(jnp.bfloat16)
+    out_ref[:, :width] = out / mass
 
     drain(spans_all.at[0, pl.ds(0, NXY - 1)], ssem.at[SPANS])
     drain(spans_all.at[0], ssem.at[OTHER])
@@ -307,7 +318,10 @@
         drain(chunk(0), ssem.at[STOP + n])
     for n in range(3):
         drain(rowx.at[n, pl.ds(0, 2 * NXY - 1)], ssem.at[ROW + n])
+    for n in range(2):
         drain(colx.at[n, pl.ds(0, NZ - 1)], ssem.at[COL + n])
+    drain(colw.at[pl.ds(0, 3)], ssem.at[COLW])
+    drain(colf.at[pl.ds(0, NA - 1)], ssem.at[COLF])
     for i, k in enumerate(ORDER):
         if k != 4:
             drain(win_in.at[pl.ds(0, len(SPREAD[k]))], ssem.at[WIN + i])
@@ -321,17 +335,12 @@
         f32, bf16 = jnp.float32, jnp.bfloat16
         target = (spans.shape[0] * mesh.size) / (centroids.shape[0] * mesh.size)
         args = [pltpu.with_memory_space_constraint(v, pltpu.HBM) for v in (spans, centroids, pattern)]
-        vmem = pl.BlockSpec(memory_space=pltpu.VMEM)
-        new, row_pot, col_pot = pl.pallas_call(
+        packed = pl.pallas_call(
             functools.partial(kernel, math.log(target), target),
             name="sinkhorn",
-            out_shape=(
-                jax.ShapeDtypeStruct((8, width), bf16),
-                jax.ShapeDtypeStruct((4, BLOCK), f32),
-                jax.ShapeDtypeStruct((4, BLOCK), f32),
-            ),
+            out_shape=jax.ShapeDtypeStruct((8, width + BLOCK), f32),
             in_specs=[pl.BlockSpec(memory_space=pltpu.HBM)] * 3,
-            out_specs=(vmem,) * 3,
+            out_specs=pl.BlockSpec(memory_space=pltpu.VMEM),
             scratch_shapes=[
                 pltpu.VMEM((2, NXY, 32, width), bf16),
                 pltpu.VMEM((NA, STRIDE, 8, width), bf16),
@@ -343,7 +352,9 @@
                 pltpu.VMEM((NA - 1, 8, width), bf16),
                 pltpu.VMEM((NA - 1, 8, width), bf16),
                 pltpu.VMEM((3, 2 * NXY, 8, BLOCK), f32),
-                pltpu.VMEM((3, NZ, 2, BLOCK), f32),
+                pltpu.VMEM((2, NZ, 2, BLOCK), f32),
+                pltpu.VMEM((4, 2, BLOCK), f32),
+                pltpu.VMEM((NA, 2, BLOCK), f32),
                 pltpu.VMEM((2, 2, BLOCK), f32),
                 pltpu.VMEM((2, BLOCK), f32),
                 pltpu.SemaphoreType.DMA((NSEM,)),
@@ -355,7 +366,8 @@
                 collective_id=0, has_side_effects=True, vmem_limit_bytes=32 * 1024 * 1024
             ),
         )(*args)
-        return new, row_pot.reshape(-1), col_pot.reshape(-1)
+        pots = packed[:, width:]
+        return packed[:, :width].astype(bf16), pots[:4].reshape(-1), pots[4:].reshape(-1)
 
     return jax.shard_map(
         per_device,

time: 107 us -> 104 us (0.972)
  Pallas kernels: 104 us -> 102 us
    pallas_call x1, Pallas kernels: 104 us -> 102 us  [per_device(): pl.pallas_call(functools.partial(kernel, math.log(target), target), name=...]
    unnamed x3 -> x0, local copies, waits for them, and re-layouts: 1.76 us -> none
where the time goes in v5:
time: 104 us; the launch traced here: 103 us
  Pallas kernels  102 us (98%)
  local copies, waits for them, and re-layouts  1.19 us (1%)
    pallas_call x1, Pallas kernels, per_device(): pl.pallas_call(functools.partial(kernel, math.log(target), target), name=...  102 us

profile of v5, /device:TPU:1, one launch (start us, length us, event | category | flops | bytes accessed | tf_op | source)
XLA Modules:
  0.0 103.4 jit_solution(15103868935594875228)
XLA Ops:
  0.6 101.6 %sinkhorn.1 = f32[8,896]{1,0:T(8,128)S(1)} custom-call(bf16[32,768]{1,0:T(8,128)(2,1)} %sp_ref.1, bf16[8,768]{1,0:T(8,128)(2,1)} %ce_ref.1, s32[4,16]{1,0:T(4,128)} %pat_ref.1), custom_call_target="tpu_custom_call" | custom-call | tf_op jit(solution)/shard_map/sinkhorn/pallas_call | solution.py:338
  102.3 0.6 slice_bitcast_fusion
  102.8 0.6 slice.20

commit v6 on v5

--- a/solution.py
+++ b/solution.py
@@ -21,8 +21,8 @@
 WINDOW = [(k, d) for k in ORDER for d in SPREAD[k]]
 SPANS, OTHER, PAT, CENT, POT, LAST = range(6)
 ROW, COL, STOP, WIN = 6, 9, 12, 19
-COLW, COLF = 27, 28
-NSEM = 29
+COLW, COLF, FAR = 27, 28, 29
+NSEM = 30
 
 
 def remote(src, dst, ssem, rsem, dev):
@@ -251,7 +251,8 @@
         last_out[i] = whole.astype(jnp.bfloat16)
         remote(last_out.at[i], last_in.at[i], ssem.at[LAST], rsem.at[LAST], z_peer(-STRIDE * k)).start()
 
-    send_last(0, 4, acc[(a + 4) % NA, b])
+    last_out[0] = acc[(a + 4) % NA, b].astype(jnp.bfloat16)
+    remote(last_out.at[0], last_in.at[0], ssem.at[FAR], rsem.at[FAR], z_peer(STRIDE * (4 * core - 2))).start()
 
     def send_window(*steps):
         for w, (k, d) in enumerate(WINDOW):
@@ -268,6 +269,8 @@
         whole = acc[(a - k + NA) % NA, b]
         for w in range(lo, lo + len(SPREAD[k])):
             whole = whole + win_in[w].astype(jnp.float32)
+        if abs(k) == 2:
+            whole = whole + jnp.where(core == (2 - k) // 4, last_in[0].astype(jnp.float32), 0.0)
         if k != 0:
             send_last(i, k, whole)
         return whole
@@ -281,6 +284,7 @@
     gather_window(3)
     gather_window(-3)
     send_window(1, -1)
+    drain(last_in.at[0], rsem.at[FAR])
     gather_window(2)
     gather_window(-2)
     send_window(0)
@@ -306,8 +310,8 @@
             line = line + jnp.sum(jnp.where(take, to_rows(pots[q, i // 2 : i // 2 + 1, :]), 0.0), axis=0, keepdims=True)
         out_ref[4 + i : 5 + i, width:] = line
 
-    drain(last_in, rsem.at[LAST])
-    out = whole + jnp.sum(last_in[...].astype(jnp.float32), axis=0)
+    drain(last_in.at[pl.ds(1, NA - 2)], rsem.at[LAST])
+    out = whole + jnp.sum(last_in[1 : NA - 1].astype(jnp.float32), axis=0)
     out_ref[:, :width] = out / mass
 
     drain(spans_all.at[0, pl.ds(0, NXY - 1)], ssem.at[SPANS])
@@ -326,7 +330,8 @@
         if k != 4:
             drain(win_in.at[pl.ds(0, len(SPREAD[k]))], ssem.at[WIN + i])
     drain(pots.at[0], ssem.at[POT])
-    drain(last_in, ssem.at[LAST])
+    drain(last_in.at[pl.ds(1, NA - 2)], ssem.at[LAST])
+    drain(last_in.at[0], ssem.at[FAR])
 
 
 def solution(mesh):

time: 104 us -> 104 us (level)
  no operation moved by 1% of the time
where the time goes in v6:
time: 104 us; the launch traced here: 103 us
  Pallas kernels  101 us (97%)
  local copies, waits for them, and re-layouts  1.19 us (1%)
    pallas_call x1, Pallas kernels, per_device(): pl.pallas_call(functools.partial(kernel, math.log(target), target), name=...  101 us

profile of v6, /device:TPU:1, one launch (start us, length us, event | category | flops | bytes accessed | tf_op | source)
XLA Modules:
  0.0 103.3 jit_solution(14596502000152901013)
XLA Ops:
  0.6 101.5 %sinkhorn.1 = f32[8,896]{1,0:T(8,128)S(1)} custom-call(bf16[32,768]{1,0:T(8,128)(2,1)} %sp_ref.1, bf16[8,768]{1,0:T(8,128)(2,1)} %ce_ref.1, s32[4,16]{1,0:T(4,128)} %pat_ref.1), custom_call_target="tpu_custom_call" | custom-call | tf_op jit(solution)/shard_map/sinkhorn/pallas_call | solution.py:343
  102.1 0.6 slice_bitcast_fusion
  102.7 0.6 slice.20
